TPU v7x, 256 devices: a whole 4x4x8 slice. The times are simulated.
256 devices in a mesh: ctx: 32 (over y, x, core), head: 8 (over z).
Axes of the slice: x: 4, y: 4, z: 8, core: 2. Of those that a mesh axis runs over, the one named last changes fastest.
Arguments:
- hidden_in: bfloat16 [8192, 2048], P('ctx'), may hold values from -6 to 6
- gain_attn: float32 [2048], replicated, may hold values from 0.1 to 1.9
- w_qkv: bfloat16 [2048, 3, 2048], P(None, None, 'head'), may hold values from -0.125 to 0.125
- conv_w: float32 [4, 3, 2048], P(None, None, 'head'), may hold values from -3 to 3
- log_decay: float32 [8192, 16], P('ctx', 'head'), may hold values from -1 to 0, as said below
- norm_gain: float32 [2048], P('head'), may hold values from 0.1 to 1.9
- w_out: bfloat16 [2048, 2048], P('head'), may hold values from -0.125 to 0.125
- gain_moe: float32 [2048], replicated, may hold values from 0.1 to 1.9
- expert_ids: int32 [8192, 8], P('ctx'), may hold values from 0 to 63, all different within a row; in each aligned block of 256 rows (0 to 255, 256 to 511, ...) at most 48 rows name the same one
- route_weights: float32 [8192, 8], P('ctx'), may hold values from 0.05 to 1
- w_gate: bfloat16 [256, 2048, 256], P(('ctx', 'head')), may hold values from -0.125 to 0.125
- w_up: bfloat16 [256, 2048, 256], P(('ctx', 'head')), may hold values from -0.125 to 0.125
- w_down: bfloat16 [256, 256, 2048], P(('ctx', 'head')), may hold values from -0.1875 to 0.1875
- grad_core: bfloat16 [8192, 2048], P('ctx', 'head'), may hold values from -6 to 6
Outputs:
- layer_out: bfloat16 [8192, 2048], P('ctx', 'head')
- grad_q: bfloat16 [8192, 2048], P('ctx', 'head')
- grad_k: bfloat16 [8192, 2048], P('ctx', 'head')
- grad_v: bfloat16 [8192, 2048], P('ctx', 'head')
Inputs may be any that keep to these rules, and one draw needn't show every extreme that they name: `expert_ids`: in each aligned block of 256 rows (the tokens of one index of ctx) no expert is chosen by more than 48 rows, a bound that some block reaches; the 8 experts of a row differ. `log_decay`: every entry is negative.
All inputs are finite; a program needn't handle non-finite values.
Results may differ from a plain program's by a relative error of at most 0.023.
Values may be sent and summed in bfloat16 or wider, within the bound.
A program may use at most 128 MiB of HBM per device.

v0:
```python
import jax
import jax.numpy as jnp
from jax import lax
from jax.sharding import PartitionSpec as P

KERNEL = 4
TOP = 8
EXP_CTX = 2


def shifted(value, axis, steps):
    count = lax.axis_size(axis)
    first, last = (max(0, -steps), min(count, count - steps))
    return lax.ppermute(value, axis, [(source, source + steps) for source in range(first, last)])


def entering(value, axis, join, neutral, backward):
    count, mine = (lax.axis_size(axis), lax.axis_index(axis))
    pieces = jax.tree.map(lambda part: lax.all_gather(part, axis), value)
    if backward:
        pieces = jax.tree.map(lambda part: part[::-1], pieces)
        mine = count - 1 - mine
    total = jax.tree.map(
        lambda part, zero: jnp.full_like(part, 0) + jnp.asarray(zero, part.dtype), value, neutral
    )

    def hop(position, total):
        longer = join(total, jax.tree.map(lambda part: part[position], pieces))
        return jax.tree.map(lambda new, old: jnp.where(position < mine, new, old), longer, total)

    return lax.fori_loop(0, count - 1, hop, total)


def rms_norm(values, gain):
    return values * lax.rsqrt(jnp.mean(values * values, axis=-1, keepdims=True) + 1e-06) * gain


def link(earlier, later):
    return (earlier[0] * later[0], later[0][:, None, None] * earlier[1] + later[1])


def body(
    hidden_in,
    gain_attn,
    w_qkv,
    conv_w,
    log_decay,
    norm_gain,
    w_out,
    gain_moe,
    expert_ids,
    route_weights,
    w_gate,
    w_up,
    w_down,
    grad_core,
):
    hi = lax.Precision.HIGHEST
    n_ctx = lax.axis_size("ctx")
    n_head = lax.axis_size("head")
    my_head = lax.axis_index("head")
    tok_dev, width = hidden_in.shape
    chans = w_qkv.shape[2]
    heads_here = log_decay.shape[1]
    head_size = chans // heads_here
    experts = EXP_CTX * n_ctx
    cap = 3 * tok_dev * TOP // (2 * experts)
    shards = n_head // EXP_CTX
    local_expert = my_head // shards
    cols = width // n_head
    x_float = hidden_in.astype(jnp.float32)
    normed = rms_norm(x_float, gain_attn).astype(jnp.bfloat16)
    mixed = jnp.einsum("ti,icj->tcj", normed, w_qkv, preferred_element_type=jnp.float32).astype(
        jnp.bfloat16
    )
    rim = shifted(mixed[tok_dev - (KERNEL - 1) :], "ctx", 1)
    padded = jnp.concatenate([rim, mixed], axis=0).astype(jnp.float32)
    conv_out = jnp.zeros(mixed.shape, jnp.float32)
    for offset in range(KERNEL):
        conv_out = (
            conv_out + conv_w[offset] * padded[KERNEL - 1 - offset : KERNEL - 1 - offset + tok_dev]
        )
    activ = jax.nn.silu(conv_out)
    shape3 = (tok_dev, heads_here, head_size)
    queries = (activ[:, 0] * head_size ** (-0.5)).astype(jnp.bfloat16).reshape(shape3)
    key_rows = activ[:, 1].astype(jnp.bfloat16).reshape(shape3)
    val_rows = activ[:, 2].astype(jnp.bfloat16).reshape(shape3)
    query_f = queries.astype(jnp.float32)
    key_f = key_rows.astype(jnp.float32)
    value_f = val_rows.astype(jnp.float32)
    cot_rows = grad_core.reshape(shape3)
    cot_f = cot_rows.astype(jnp.float32)
    cum_decay = jnp.cumsum(log_decay, axis=0)
    cum_t = cum_decay.T
    diff = cum_t[:, :, None] - cum_t[:, None, :]
    lower = (jnp.arange(tok_dev)[:, None] >= jnp.arange(tok_dev)[None, :])[None]
    decay_mask = jnp.where(lower, jnp.exp(jnp.where(lower, diff, 0.0)), 0.0)
    scores = (
        jnp.einsum("thd,shd->hts", queries, key_rows, preferred_element_type=jnp.float32)
        * decay_mask
    )
    tail = jnp.exp(cum_decay[-1][None, :] - cum_decay)
    lead_decay = jnp.exp(cum_decay)
    summary = jnp.einsum("shd,she->hde", key_f * tail[:, :, None], value_f, precision=hi)
    backsum = jnp.einsum("thd,the->hde", query_f * lead_decay[:, :, None], cot_f, precision=hi)
    zeros_state = jnp.zeros((heads_here, head_size, head_size), jnp.float32)
    block_decay = jnp.exp(cum_decay[-1])
    identity = (jnp.ones((heads_here,), jnp.float32), zeros_state)
    _, state_in = entering((block_decay, summary), "ctx", link, identity, False)
    _, grad_in = entering((block_decay, backsum), "ctx", link, identity, True)
    local = jnp.einsum("hts,shd->thd", scores, value_f, precision=hi)
    carried = jnp.einsum("thd,hde->the", query_f, state_in, precision=hi) * lead_decay[:, :, None]
    attended = local + carried
    dov = (
        jnp.einsum("thd,shd->hts", cot_rows, val_rows, preferred_element_type=jnp.float32)
        * decay_mask
    )
    grad_q = jnp.einsum("hts,shd->thd", dov, key_f, precision=hi)
    grad_q = grad_q + lead_decay[:, :, None] * jnp.einsum(
        "the,hde->thd", cot_f, state_in, precision=hi
    )
    grad_k = jnp.einsum("hts,thd->shd", dov, query_f, precision=hi)
    grad_k = grad_k + tail[:, :, None] * jnp.einsum("the,hde->thd", value_f, grad_in, precision=hi)
    grad_v = jnp.einsum("hts,the->she", scores, cot_f, precision=hi)
    grad_v = grad_v + tail[:, :, None] * jnp.einsum("thd,hde->the", key_f, grad_in, precision=hi)
    headed = rms_norm(attended, norm_gain.reshape(heads_here, head_size)).reshape(tok_dev, chans)
    headed = headed.astype(jnp.bfloat16)
    partial_out = jnp.dot(headed, w_out, preferred_element_type=jnp.float32)
    attn_total = lax.psum(partial_out.astype(jnp.bfloat16), "head").astype(jnp.float32)
    resid_full = x_float + attn_total
    moe_in = rms_norm(resid_full, gain_moe).astype(jnp.bfloat16)
    resid_mine = lax.dynamic_slice_in_dim(resid_full, my_head * cols, cols, 1)
    hot = (expert_ids[:, :, None] == jnp.arange(experts, dtype=jnp.int32)).astype(jnp.int32)
    counts = jnp.sum(hot, axis=1)
    ranks = jnp.cumsum(counts, axis=0) - counts
    slot = jnp.sum(hot * ranks[:, None, :], axis=-1)
    owner = expert_ids // EXP_CTX
    local_id = expert_ids % EXP_CTX
    picked = local_id == local_expert
    source_rows = jnp.broadcast_to(moe_in[:, None, :], (tok_dev, TOP, width)).reshape(-1, width)
    total = jnp.zeros((tok_dev, width), jnp.float32)
    positions = jnp.where(picked, owner * cap + slot, n_ctx * cap).reshape(-1)
    buffer = (
        jnp.zeros((n_ctx * cap, width), jnp.bfloat16).at[positions].set(source_rows, mode="drop")
    )
    buffer = buffer.reshape(n_ctx, cap, width)
    batch = lax.all_to_all(buffer, "ctx", split_axis=0, concat_axis=0, tiled=True)
    gate_val = jnp.einsum("ncd,df->ncf", batch, w_gate[0], preferred_element_type=jnp.float32)
    up_val = jnp.einsum("ncd,df->ncf", batch, w_up[0], preferred_element_type=jnp.float32)
    inner = (jax.nn.silu(gate_val) * up_val).astype(jnp.bfloat16)
    returned = lax.all_to_all(
        jnp.einsum("ncf,fd->ncd", inner, w_down[0], preferred_element_type=jnp.float32).astype(
            jnp.bfloat16
        ),
        "ctx",
        split_axis=0,
        concat_axis=0,
        tiled=True,
    )
    flat_back = returned.reshape(n_ctx * cap, width)
    fetch = jnp.where(picked, owner * cap + slot, 0)
    weights = jnp.where(picked, route_weights, 0.0)
    for chosen in range(TOP):
        total = total + weights[:, chosen, None] * flat_back[fetch[:, chosen]].astype(jnp.float32)
    moe_out = lax.psum_scatter(
        total.astype(jnp.bfloat16), "head", scatter_dimension=1, tiled=True
    ).astype(jnp.float32)
    layer_out = (resid_mine + moe_out).astype(jnp.bfloat16)
    return (
        layer_out,
        grad_q.reshape(tok_dev, chans).astype(jnp.bfloat16),
        grad_k.reshape(tok_dev, chans).astype(jnp.bfloat16),
        grad_v.reshape(tok_dev, chans).astype(jnp.bfloat16),
    )


def solution(mesh):
    in_specs = (
        P("ctx", None),
        P(),
        P(None, None, "head"),
        P(None, None, "head"),
        P("ctx", "head"),
        P("head"),
        P("head", None),
        P(),
        P("ctx", None),
        P("ctx", None),
        P(("ctx", "head"), None, None),
        P(("ctx", "head"), None, None),
        P(("ctx", "head"), None, None),
        P("ctx", "head"),
    )
    out_specs = (P("ctx", "head"), P("ctx", "head"), P("ctx", "head"), P("ctx", "head"))
    return jax.shard_map(body, mesh=mesh, in_specs=in_specs, out_specs=out_specs, check_vma=False)
```

profile of v0, /device:TPU:32, one launch (start us, length us, event | category | flops | bytes accessed | tf_op | source)
XLA Modules:
  0.0 524.5 jit_solution(18386399533522410628)
XLA Ops:
  7.2 1.7 fusion.6
  9.4 2.3 convolution_convert_fusion.2
  12.4 1.7 collective-permute-start
  15.5 1.1 maximum_convert_fusion
  18.4 25.0 %all-gather.2 = f32[32,1,2]{2,1,0:T(1,128)S(1)} all-gather(f32[1,1,2]{2,1,0:T(1,128)S(1)} %bitcast.218), channel_id=1, replica_groups=mesh['ctx'=32,'head'=8] {'ctx'}, dimensions={0}, use_global_device_ids=true | all-gather | bytes 264 | tf_op jit(solution)/shard_map/all_gather | solution.py:19
  45.1 29.0 %all-gather.6.cloned.1.call-done = f32[64,128,128]{2,1,0:T(8,128)} async-done(((f32[2,128,128]{2,1,0:T(8,128)}), f32[64,128,128]{2,1,0:T(8,128)}) %all-gather.6.cloned.1.call-update) | async-done | bytes 4194320 | tf_op jit(solution)/shard_map/all_gather | solution.py:19
  74.0 32.2 %while.28 = (s32[]{:T(128)}, f32[2,128,128]{2,1,0:T(8,128)S(1)}, s32[]{:T(128)}, f32[32,2]{1,0:T(8,128)S(1)}, f32[32,2,128,128]{3,2,1,0:T(8,128)}, /*index=5*/s32[]{:T(128)}, s32[]{:T(128)}) while((s32[]{:T(128)}, f32[2,128,128]{2,1,0:T(8,128)S(1)}, s32[]{:T(128)}, f32[32,2]{1,0:T(8,128)S(1)}, f32[32,2,128,128]{3,2,1,0:T(8,128)}, ...), condition=%wide.region_4.5_spmd.clone, body=%wide.region_3.4_spmd.clone.sunk | while | flops 131076 | bytes 393353 | solution.py:31
  74.0 1.1 fusion.86
  75.2 1.0 fusion.86
  76.2 1.0 fusion.86
  77.2 1.0 fusion.86
  78.3 1.0 fusion.86
  79.3 1.0 fusion.86
  80.3 1.0 fusion.86
  81.4 1.0 fusion.86
  82.4 1.0 fusion.86
  83.5 1.0 fusion.86
  84.5 1.0 fusion.86
  85.5 1.0 fusion.86
  86.6 1.0 fusion.86
  87.6 1.0 fusion.86
  88.6 1.0 fusion.86
  89.7 1.0 fusion.86
  90.7 1.0 fusion.86
  91.8 1.0 fusion.86
  92.8 1.0 fusion.86
  93.8 1.0 fusion.86
  94.9 1.0 fusion.86
  95.9 1.0 fusion.86
  97.0 1.0 fusion.86
  98.0 1.0 fusion.86
  99.0 1.0 fusion.86
  100.1 1.0 fusion.86
  101.1 1.0 fusion.86
  102.1 1.0 fusion.86
  103.2 1.0 fusion.86
  104.2 1.0 fusion.86
  107.3 1.4 convolution_convert_fusion.1
  110.4 73.6 %all-reduce.2.cloned.1.call-done = bf16[256,2048]{1,0:T(8,128)(2,1)} async-done(((bf16[256,2048]{1,0:T(8,128)(2,1)}), bf16[256,2048]{1,0:T(8,128)(2,1)}) %all-reduce.2.cloned.1.call-update) | async-done | bytes 1048592 | tf_op jit(solution)/shard_map/psum | solution.py:129
  184.0 3.0 convert_add_fusion
  187.5 16.4 %scatter_custom_fusion = bf16[1536,2048]{1,0:T(8,128)(2,1)} fusion(s32[2048]{0:T(1024)} %bitcast.196, bf16[256,2048]{1,0:T(8,128)(2,1)S(1)} %multiply_convert_fusion, bf16[]{:T(256)} %constant.131.clone.1), kind=kCustom, calls=%fused_computation.15 | custom fusion | bytes 7340544 | tf_op jit(solution)/shard_map/scatter | solution.py:144
  203.9 7.4 %all-to-all-start = ((bf16[32,48,2048]{2,1,0:T(8,128)(2,1)}), bf16[32,48,2048]{2,1,0:T(8,128)(2,1)}, u32[]{:S(2)}, u32[]{:S(2)}) async-start(bf16[32,48,2048]{2,1,0:T(8,128)(2,1)} %bitcast.179), calls=%async_computation | async-start | bytes 12582912 | tf_op jit(solution)/shard_map/all_to_all | solution.py:147
  212.5 81.7 %all-to-all-done = bf16[32,48,2048]{2,1,0:T(8,128)(2,1)} async-done(((bf16[32,48,2048]{2,1,0:T(8,128)(2,1)}), bf16[32,48,2048]{2,1,0:T(8,128)(2,1)}, u32[]{:S(2)}, u32[]{:S(2)}) %all-to-all-start) | async-done | bytes 6291488 | tf_op jit(solution)/shard_map/all_to_all | solution.py:147
  294.1 5.9 %fusion.26 = f32[32,48,256]{2,1,0:T(8,128)} fusion(bf16[32,48,2048]{2,1,0:T(8,128)(2,1)} %all-to-all-done, bf16[1,2048,256]{2,1,0:T(8,128)(2,1)S(1)} %copy-done.30), kind=kOutput, calls=%fused_computation.57 | convolution fusion | flops 1610612736 | bytes 8912896 | tf_op jit(solution)/shard_map/ncd,df->ncf/dot_general | solution.py:148
  300.1 12.6 %convolution_convert_fusion = bf16[32,48,2048]{2,1,0:T(8,128)(2,1)} fusion(f32[32,48,256]{2,1,0:T(8,128)} %fusion.26, bf16[32,48,2048]{2,1,0:T(8,128)(2,1)} %all-to-all-done, bf16[1,256,2048]{2,1,0:T(8,128)(2,1)S(1)} %copy-done.31, bf16[1,2048,256]{2,1,0:T(8,128)(2,1)} %param.29), kind=kOutput, calls=%fused_computation.17 | convolution fusion | flops 3226730496 | bytes 16252928 | tf_op jit(solution)/shard_map/ncf,fd->ncd/dot_general | solution.py:152
  312.7 5.0 all-to-all-start.1
  321.8 1.1 fusion.9
  322.9 4.6 rev.7
  327.5 68.1 %all-to-all-done.1 = bf16[32,48,2048]{2,1,0:T(8,128)(2,1)} async-done(((bf16[32,48,2048]{2,1,0:T(8,128)(2,1)}), bf16[32,48,2048]{2,1,0:T(8,128)(2,1)}, u32[]{:S(2)}, u32[]{:S(2)}) %all-to-all-start.1) | async-done | bytes 6291488 | tf_op jit(solution)/shard_map/all_to_all | solution.py:151
  395.6 6.0 %gather_fusion.7 = bf16[256,2048]{1,0:T(8,128)(2,1)S(1)} fusion(bf16[1536,2048]{1,0:T(8,128)(2,1)} %bitcast.21, s32[1024]{0:T(1024)S(1)} %pad_clamp_fusion), kind=kCustom, calls=%fused_computation.7 | custom fusion | bytes 2098176 | tf_op jit(solution)/shard_map/gather | solution.py:164
  401.6 6.0 %gather_fusion.6 = bf16[256,2048]{1,0:T(8,128)(2,1)S(1)} fusion(bf16[1536,2048]{1,0:T(8,128)(2,1)} %bitcast.21, s32[1024]{0:T(1024)S(1)} %pad_clamp_fusion.1), kind=kCustom, calls=%fused_computation.6 | custom fusion | bytes 2098176 | tf_op jit(solution)/shard_map/gather | solution.py:164
  407.6 6.0 %gather_fusion.5 = bf16[256,2048]{1,0:T(8,128)(2,1)S(1)} fusion(bf16[1536,2048]{1,0:T(8,128)(2,1)} %bitcast.21, s32[1024]{0:T(1024)S(1)} %pad_clamp_fusion.2), kind=kCustom, calls=%fused_computation.5 | custom fusion | bytes 2098176 | tf_op jit(solution)/shard_map/gather | solution.py:164
  413.5 7.1 %gather_fusion.4 = bf16[256,2048]{1,0:T(8,128)(2,1)} fusion(bf16[1536,2048]{1,0:T(8,128)(2,1)} %bitcast.21, s32[1024]{0:T(1024)} %pad_clamp_fusion.3), kind=kCustom, calls=%fused_computation.4 | custom fusion | bytes 2098176 | tf_op jit(solution)/shard_map/gather | solution.py:164
  420.6 7.3 %gather_fusion.3 = bf16[256,2048]{1,0:T(8,128)(2,1)} fusion(bf16[1536,2048]{1,0:T(8,128)(2,1)} %bitcast.21, s32[1024]{0:T(1024)} %pad_clamp_fusion.4), kind=kCustom, calls=%fused_computation.3 | custom fusion | bytes 2098176 | tf_op jit(solution)/shard_map/gather | solution.py:164
  427.9 7.1 %gather_fusion.2 = bf16[256,2048]{1,0:T(8,128)(2,1)} fusion(bf16[1536,2048]{1,0:T(8,128)(2,1)} %bitcast.21, s32[1024]{0:T(1024)} %pad_clamp_fusion.5), kind=kCustom, calls=%fused_computation.2 | custom fusion | bytes 2098176 | tf_op jit(solution)/shard_map/gather | solution.py:164
  435.0 7.1 %gather_fusion.1 = bf16[256,2048]{1,0:T(8,128)(2,1)} fusion(bf16[1536,2048]{1,0:T(8,128)(2,1)} %bitcast.21, s32[1024]{0:T(1024)} %pad_clamp_fusion.6), kind=kCustom, calls=%fused_computation.1 | custom fusion | bytes 2098176 | tf_op jit(solution)/shard_map/gather | solution.py:164
  442.0 7.0 %gather_fusion = bf16[256,2048]{1,0:T(8,128)(2,1)} fusion(bf16[1536,2048]{1,0:T(8,128)(2,1)} %bitcast.21, s32[1024]{0:T(1024)S(1)} %pad_clamp_fusion.7), kind=kCustom, calls=%fused_computation | custom fusion | bytes 2098176 | tf_op jit(solution)/shard_map/gather | solution.py:164
  449.0 4.6 add_convert_fusion
  453.7 52.9 %while.29 = (s32[]{:T(128)}, f32[2,128,128]{2,1,0:T(8,128)S(1)}, s32[]{:T(128)}, f32[32,2]{1,0:T(8,128)}, f32[32,2,128,128]{3,2,1,0:T(8,128)}, /*index=5*/s32[]{:T(128)}, s32[]{:T(128)}) while((s32[]{:T(128)}, f32[2,128,128]{2,1,0:T(8,128)S(1)}, s32[]{:T(128)}, f32[32,2]{1,0:T(8,128)}, f32[32,2,128,128]{3,2,1,0:T(8,128)}, ...), condition=%wide.region_15.16_spmd.clone, body=%wide.region_14.15_spmd.clone.sunk | while | flops 131076 | bytes 393353 | solution.py:31
  508.0 1.8 copy.199
  509.8 1.2 fusion.16
  511.0 1.5 fusion.18
  513.6 1.5 fusion.19
  515.8 1.7 add_convert_fusion.1
  (235 shorter events, 70.7 us)
Async XLA Ops:
  7.2 2.2 copy-start
  7.2 66.8 %all-gather.6.cloned.1.call-start = ((), (), s32[]{:S(2)}) async-start(), calls=%async_computation.5 | async-start | bytes 4325376 | tf_op jit(solution)/shard_map/all_gather | solution.py:19
  9.4 4.8 copy-start.28
  9.4 6.0 %copy-start.19 = (f32[4,3,256]{2,0,1:T(4,128)S(1)}, f32[4,3,256]{2,0,1:T(4,128)}, u32[]{:S(2)}) copy-start(f32[4,3,256]{2,0,1:T(4,128)} %param.21) | copy-start | bytes 36868
  11.7 0.7 copy-start.13
  12.4 3.1 collective-permute-start
  15.2 29.5 %copy-start.25 = (f32[1,2,2,128]{3,1,2,0:T(2,128)}, f32[1,2,2,128]{3,1,2,0:T(2,128)S(1)}, u32[]{:S(2)}) copy-start(f32[1,2,2,128]{3,1,2,0:T(2,128)S(1)} %copy.239) | copy-start | bytes 6148
  16.6 27.0 %copy-start.14 = (s32[256,8]{0,1:T(8,128)S(1)}, s32[256,8]{0,1:T(8,128)}, u32[]{:S(2)}) copy-start(s32[256,8]{0,1:T(8,128)} %param.26) | copy-start | bytes 24580
  17.2 56.8 %copy-start.9 = (bf16[256,2,128]{2,1,0:T(2,128)(2,1)}, bf16[256,2,128]{2,1,0:T(2,128)(2,1)S(1)}, u32[]{:S(2)}) copy-start(bf16[256,2,128]{2,1,0:T(2,128)(2,1)S(1)} %convert_element_type.119) | copy-start | bytes 393220
  17.4 27.2 %copy-start.11 = (bf16[256,2,128]{0,2,1:T(8,128)(2,1)}, bf16[256,2,128]{0,2,1:T(8,128)(2,1)S(1)}, u32[]{:S(2)}) copy-start(bf16[256,2,128]{0,2,1:T(8,128)(2,1)S(1)} %copy.176) | copy-start | bytes 393220
  18.3 165.6 %all-reduce.2.cloned.1.call-start = ((), (), s32[]{:S(2)}) async-start(), calls=%async_computation.3 | async-start | bytes 2097152 | tf_op jit(solution)/shard_map/psum | solution.py:129
  43.5 30.5 %copy-start.20 = (f32[32,1,2]{0,2,1:T(2,128)}, f32[32,1,2]{0,2,1:T(2,128)S(1)}, u32[]{:S(2)}) copy-start(f32[32,1,2]{0,2,1:T(2,128)S(1)} %copy.175) | copy-start | bytes 772
  44.5 62.1 %copy-start.24 = (s32[64,3]{0,1:T(4,128)}, s32[64,3]{0,1:T(4,128)S(1)}, u32[]{:S(2)}) copy-start(s32[64,3]{0,1:T(4,128)S(1)} %reduce-window.19) | copy-start | bytes 2308
  44.6 62.0 %copy-start.16 = (pred[256,256]{1,0:T(8,128)(4,1)}, pred[256,256]{1,0:T(8,128)(4,1)S(1)}, u32[]{:S(2)}) copy-start(pred[256,256]{1,0:T(8,128)(4,1)S(1)} %iota_compare_fusion.1) | copy-start | bytes 196612
  44.7 166.8 %copy-start.6 = (bf16[256,1,256]{0,2,1:T(8,128)(2,1)}, bf16[256,1,256]{0,2,1:T(8,128)(2,1)S(1)}, u32[]{:S(2)}) copy-start(bf16[256,1,256]{0,2,1:T(8,128)(2,1)S(1)} %copy.207) | copy-start | bytes 393220
  45.0 62.1 %copy-start.4 = (f32[2,256,256]{2,1,0:T(8,128)}, f32[2,256,256]{2,1,0:T(8,128)S(1)}, u32[]{:S(2)}) copy-start(f32[2,256,256]{2,1,0:T(8,128)S(1)} %convolution_multiply_fusion) | copy-start | bytes 1572868
  45.0 62.1 %copy-start.29 = (f32[256]{0:T(256)S(1)}, f32[256]{0:T(256)}, u32[]{:S(2)}) copy-start(f32[256]{0:T(256)} %param.23) | copy-start | bytes 3076
  74.0 33.2 %copy-start.12 = (bf16[256,2048]{1,0:T(8,128)(2,1)S(1)}, bf16[256,2048]{1,0:T(8,128)(2,1)}, u32[]{:S(2)}) copy-start(bf16[256,2048]{1,0:T(8,128)(2,1)} %param.24) | copy-start | bytes 3145732
  107.1 1.7 slice-start
  107.1 1.8 copy-start.23
  107.1 76.9 %copy-start.2 = (bf16[256,2048]{1,0:T(8,128)(2,1)S(1)}, bf16[256,2048]{1,0:T(8,128)(2,1)}, u32[]{:S(2)}) copy-start(bf16[256,2048]{1,0:T(8,128)(2,1)} %param.18) | copy-start | bytes 3145732
  184.0 3.0 copy-start.3
  184.0 3.0 copy-start.22
  203.9 7.4 %copy-start.15 = (bf16[256,256]{1,0:T(8,128)(2,1)S(1)}, bf16[256,256]{1,0:T(8,128)(2,1)}, u32[]{:S(2)}) copy-start(bf16[256,256]{1,0:T(8,128)(2,1)} %param.31) | copy-start | bytes 393220
  203.9 90.2 %copy-start.30 = (bf16[1,2048,256]{2,1,0:T(8,128)(2,1)S(1)}, bf16[1,2048,256]{2,1,0:T(8,128)(2,1)}, u32[]{:S(2)}) copy-start(bf16[1,2048,256]{2,1,0:T(8,128)(2,1)} %param.28) | copy-start | bytes 3145732
  203.9 90.2 %all-to-all-start = ((bf16[32,48,2048]{2,1,0:T(8,128)(2,1)}), bf16[32,48,2048]{2,1,0:T(8,128)(2,1)}, u32[]{:S(2)}, u32[]{:S(2)}) async-start(bf16[32,48,2048]{2,1,0:T(8,128)(2,1)} %bitcast.179), calls=%async_computation | async-start | bytes 12582912 | tf_op jit(solution)/shard_map/all_to_all | solution.py:147
  211.3 111.6 %all-gather.8.cloned.1.call-start = ((), (), s32[]{:S(2)}) async-start(), calls=%async_computation.6 | async-start | bytes 4325376 | tf_op jit(solution)/shard_map/all_gather | solution.py:19
  211.5 110.4 %copy-start.7 = (bf16[256,256]{0,1:T(8,128)(2,1)}, bf16[256,256]{0,1:T(8,128)(2,1)S(1)}, u32[]{:S(2)}) copy-start(bf16[256,256]{0,1:T(8,128)(2,1)S(1)} %copy.208) | copy-start | bytes 393220
  212.4 87.6 %copy-start.31 = (bf16[1,256,2048]{2,1,0:T(8,128)(2,1)S(1)}, bf16[1,256,2048]{2,1,0:T(8,128)(2,1)}, u32[]{:S(2)}) copy-start(bf16[1,256,2048]{2,1,0:T(8,128)(2,1)} %param.30) | copy-start | bytes 3145732
  312.7 5.3 %copy-start.21 = (f32[32,1,2]{0,2,1:T(2,128)S(1)}, f32[32,1,2]{0,2,1:T(2,128)}, u32[]{:S(2)}) copy-start(f32[32,1,2]{0,2,1:T(2,128)} %copy-done.20) | copy-start | bytes 772
  312.7 8.5 %copy-start.18 = (f32[256,8]{0,1:T(8,128)S(1)}, f32[256,8]{0,1:T(8,128)}, u32[]{:S(2)}) copy-start(f32[256,8]{0,1:T(8,128)} %get-tuple-element.336) | copy-start | bytes 24580
  312.7 9.1 %copy-start.17 = (pred[256,256]{1,0:T(8,128)(4,1)S(1)}, pred[256,256]{1,0:T(8,128)(4,1)}, u32[]{:S(2)}) copy-start(pred[256,256]{1,0:T(8,128)(4,1)} %copy-done.16) | copy-start | bytes 196612
  312.7 9.1 %copy-start.26 = (f32[1,2,2,128]{3,1,2,0:T(2,128)S(1)}, f32[1,2,2,128]{3,1,2,0:T(2,128)}, u32[]{:S(2)}) copy-start(f32[1,2,2,128]{3,1,2,0:T(2,128)} %copy-done.25) | copy-start | bytes 6148
  312.7 83.0 %all-to-all-start.1 = ((bf16[32,48,2048]{2,1,0:T(8,128)(2,1)}), bf16[32,48,2048]{2,1,0:T(8,128)(2,1)}, u32[]{:S(2)}, u32[]{:S(2)}) async-start(bf16[32,48,2048]{2,1,0:T(8,128)(2,1)} %convolution_convert_fusion), calls=%async_computation.1 | async-start | bytes 12582912 | tf_op jit(solution)/shard_map/all_to_all | solution.py:151
  317.7 198.0 %reduce-scatter.2.cloned.1.call-start = ((), (), s32[]{:S(2)}) async-start(), calls=%async_computation.4 | async-start | bytes 1179648 | tf_op jit(solution)/shard_map/reduce_scatter | solution.py:165
  442.0 7.0 %copy-start.27 = (f32[256,1]{0,1:T(1,128)S(1)}, f32[256,1]{0,1:T(1,128)}, u32[]{:S(2)}) copy-start(f32[256,1]{0,1:T(1,128)} %get-tuple-element.350) | copy-start | bytes 3076
  453.6 53.0 %copy-start.10 = (bf16[256,2,128]{2,1,0:T(2,128)(2,1)S(1)}, bf16[256,2,128]{2,1,0:T(2,128)(2,1)}, u32[]{:S(2)}) copy-start(bf16[256,2,128]{2,1,0:T(2,128)(2,1)} %copy-done.9) | copy-start | bytes 393220
  453.6 53.3 %copy-start.5 = (f32[2,256,256]{2,1,0:T(8,128)S(1)}, f32[2,256,256]{2,1,0:T(8,128)}, u32[]{:S(2)}) copy-start(f32[2,256,256]{2,1,0:T(8,128)} %copy-done.4) | copy-start | bytes 1572868
  453.6 53.3 %copy-start.8 = (bf16[256,256]{0,1:T(8,128)(2,1)S(1)}, bf16[256,256]{0,1:T(8,128)(2,1)}, u32[]{:S(2)}) copy-start(bf16[256,256]{0,1:T(8,128)(2,1)} %copy-done.7) | copy-start | bytes 393220
  508.0 9.5 %copy-start.1 = (bf16[2048,3,256]{2,0,1:T(8,128)(2,1)S(1)}, bf16[2048,3,256]{2,0,1:T(8,128)(2,1)}, u32[]{:S(2)}) copy-start(bf16[2048,3,256]{2,0,1:T(8,128)(2,1)} %param.20) | copy-start | bytes 9437188
Sparse Core Ops, SparseCore 0:
  18.5 55.5 all-gather.5
  108.9 75.0 all-reduce.1
  215.3 86.4 all-gather.7
  453.8 31.1 reduce-scatter.1
where the time goes:
time: 535 us; the launch traced here: 524 us
  waiting for transfers between devices  252 us (47%)
  local copies, waits for them, and re-layouts  104 us (19%)
  other arithmetic  80.3 us (15%)
  matrix products  32 us (6%)
  blocking collectives  25 us (5%)
  between operations  14.9 us (3%)
  starting transfers between devices  14.4 us (3%)
    all_to_all x1, waiting for transfers between devices, body(): lax.all_to_all(buffer, 'ctx', split_axis=0, concat_axis=0, tiled=True)  81.7 us
    psum x1, waiting for transfers between devices, body(): lax.psum(partial_out.astype(jnp.bfloat16), 'head').astype(jnp.float32)  73.6 us
    all_to_all x1, waiting for transfers between devices, body(): lax.all_to_all(jnp.einsum('ncf,fd->ncd', inner, w_down[0], preferred_elem...  68.1 us
    select_n x62, other arithmetic, hop(): jnp.where(position < mine, new, old)  61.6 us
    gather x8, local copies, waits for them, and re-layouts, body(): flat_back[fetch[:, chosen]].astype(jnp.float32)  53.3 us
    all_gather x2, waiting for transfers between devices, entering(): pieces = jax.tree.map(lambda part: lax.all_gather(part, axis), value)  29 us
    all_gather x1, blocking collectives, entering(): pieces = jax.tree.map(lambda part: lax.all_gather(part, axis), value)  25 us
    mul x62, local copies, waits for them, and re-layouts, link(): later[0][:, None, None] * earlier[1] + later[1]  21.8 us
  transfers between devices with their start and end apart: 7, of which 4 were waited for; matrix products, arithmetic and copies ran while one was open for 18% of the time, Pallas kernels for 0%

commit v1 on v0

--- a/solution.py
+++ b/solution.py
@@ -126,7 +126,9 @@
     headed = rms_norm(attended, norm_gain.reshape(heads_here, head_size)).reshape(tok_dev, chans)
     headed = headed.astype(jnp.bfloat16)
     partial_out = jnp.dot(headed, w_out, preferred_element_type=jnp.float32)
-    attn_total = lax.psum(partial_out.astype(jnp.bfloat16), "head").astype(jnp.float32)
+    attn_total = jnp.sum(lax.all_gather(partial_out.astype(jnp.bfloat16), "head"), axis=0).astype(
+        jnp.float32
+    )
     resid_full = x_float + attn_total
     moe_in = rms_norm(resid_full, gain_moe).astype(jnp.bfloat16)
     resid_mine = lax.dynamic_slice_in_dim(resid_full, my_head * cols, cols, 1)

time: 535 us -> 551 us (1.030)
  waiting for transfers between devices: 252 us -> 266 us
    all_gather x0 -> x1, waiting for transfers between devices: none -> 89.3 us  [body(): lax.all_gather(partial_out.astype(jnp.bfloat16), 'head')]
    psum x1 -> x0, waiting for transfers between devices: 73.6 us -> none  [body(): lax.psum(partial_out.astype(jnp.bfloat16), 'head').astype(jnp.float32)]
  transfers between devices with their start and end apart: 7 -> 7, of which waited for: 4 -> 4; matrix products, arithmetic and copies ran while one was open for 18% -> 17% of each run, Pallas kernels for 0% -> 0%
where the time goes in v1:
time: 551 us; the launch traced here: 543 us
  waiting for transfers between devices  266 us (48%)
  local copies, waits for them, and re-layouts  104 us (19%)
  other arithmetic  84.3 us (15%)
  matrix products  32.4 us (6%)
  blocking collectives  25.6 us (5%)
  between operations  14.9 us (3%)
  starting transfers between devices  14.7 us (3%)
    all_gather x1, waiting for transfers between devices, body(): lax.all_gather(partial_out.astype(jnp.bfloat16), 'head')  89.3 us
    all_to_all x1, waiting for transfers between devices, body(): lax.all_to_all(buffer, 'ctx', split_axis=0, concat_axis=0, tiled=True)  79.4 us
    all_to_all x1, waiting for transfers between devices, body(): lax.all_to_all(jnp.einsum('ncf,fd->ncd', inner, w_down[0], preferred_elem...  68 us
    select_n x62, other arithmetic, hop(): jnp.where(position < mine, new, old)  61.6 us
    gather x8, local copies, waits for them, and re-layouts, body(): flat_back[fetch[:, chosen]].astype(jnp.float32)  53.4 us
    all_gather x2, waiting for transfers between devices, entering(): pieces = jax.tree.map(lambda part: lax.all_gather(part, axis), value)  28.8 us
    all_gather x1, blocking collectives, entering(): pieces = jax.tree.map(lambda part: lax.all_gather(part, axis), value)  25.6 us
    mul x62, local copies, waits for them, and re-layouts, link(): later[0][:, None, None] * earlier[1] + later[1]  21.7 us
  transfers between devices with their start and end apart: 7, of which 4 were waited for; matrix products, arithmetic and copies ran while one was open for 17% of the time, Pallas kernels for 0%

profile of v1, /device:TPU:32, one launch (start us, length us, event | category | flops | bytes accessed | tf_op | source)
XLA Modules:
  0.0 542.9 jit_solution(14343354105941075919)
XLA Ops:
  7.2 1.7 fusion.6
  9.4 2.3 convolution_convert_fusion.2
  12.4 1.7 collective-permute-start
  15.5 1.1 maximum_convert_fusion
  18.4 25.6 %all-gather.3 = f32[32,1,2]{2,1,0:T(1,128)S(1)} all-gather(f32[1,1,2]{2,1,0:T(1,128)S(1)} %bitcast.220), channel_id=1, replica_groups=mesh['ctx'=32,'head'=8] {'ctx'}, dimensions={0}, use_global_device_ids=true | all-gather | bytes 264 | tf_op jit(solution)/shard_map/all_gather | solution.py:19
  45.2 28.7 %all-gather.8.cloned.1.call-done = f32[64,128,128]{2,1,0:T(8,128)} async-done(((f32[2,128,128]{2,1,0:T(8,128)}), f32[64,128,128]{2,1,0:T(8,128)}) %all-gather.8.cloned.1.call-update) | async-done | bytes 4194320 | tf_op jit(solution)/shard_map/all_gather | solution.py:19
  74.0 32.2 %while.28 = (s32[]{:T(128)}, f32[2,128,128]{2,1,0:T(8,128)S(1)}, s32[]{:T(128)}, f32[32,2]{1,0:T(8,128)S(1)}, f32[32,2,128,128]{3,2,1,0:T(8,128)}, /*index=5*/s32[]{:T(128)}, s32[]{:T(128)}) while((s32[]{:T(128)}, f32[2,128,128]{2,1,0:T(8,128)S(1)}, s32[]{:T(128)}, f32[32,2]{1,0:T(8,128)S(1)}, f32[32,2,128,128]{3,2,1,0:T(8,128)}, ...), condition=%wide.region_4.5_spmd.clone, body=%wide.region_3.4_spmd.clone.sunk | while | flops 131076 | bytes 393353 | solution.py:31
  74.0 1.1 fusion.86
  75.1 1.0 fusion.86
  76.2 1.0 fusion.86
  77.2 1.0 fusion.86
  78.2 1.0 fusion.86
  79.3 1.0 fusion.86
  80.3 1.0 fusion.86
  81.3 1.0 fusion.86
  82.4 1.0 fusion.86
  83.4 1.0 fusion.86
  84.5 1.0 fusion.86
  85.5 1.0 fusion.86
  86.5 1.0 fusion.86
  87.6 1.0 fusion.86
  88.6 1.0 fusion.86
  89.6 1.0 fusion.86
  90.7 1.0 fusion.86
  91.7 1.0 fusion.86
  92.8 1.0 fusion.86
  93.8 1.0 fusion.86
  94.8 1.0 fusion.86
  95.9 1.0 fusion.86
  96.9 1.0 fusion.86
  98.0 1.0 fusion.86
  99.0 1.0 fusion.86
  100.0 1.0 fusion.86
  103.1 1.0 fusion.86
  104.2 1.0 fusion.86
  107.2 1.5 convolution_convert_fusion.1
  111.3 89.3 %all-gather.10.cloned.1.call-done = bf16[2048,2048]{1,0:T(8,128)(2,1)} async-done(((bf16[256,2048]{1,0:T(8,128)(2,1)}), bf16[2048,2048]{1,0:T(8,128)(2,1)}) %all-gather.10.cloned.1.call-update) | async-done | bytes 8388624 | tf_op jit(solution)/shard_map/all_gather | solution.py:129
  200.7 5.3 reduce_sum.59
  206.0 1.7 convert_add_fusion
  208.2 15.9 %scatter_custom_fusion = bf16[1536,2048]{1,0:T(8,128)(2,1)} fusion(s32[2048]{0:T(1024)} %bitcast.198, bf16[256,2048]{1,0:T(8,128)(2,1)S(1)} %multiply_convert_fusion, bf16[]{:T(256)} %constant.125.clone.1), kind=kCustom, calls=%fused_computation.15 | custom fusion | bytes 7340544 | tf_op jit(solution)/shard_map/scatter | solution.py:146
  224.1 7.3 %all-to-all-start = ((bf16[32,48,2048]{2,1,0:T(8,128)(2,1)}), bf16[32,48,2048]{2,1,0:T(8,128)(2,1)}, u32[]{:S(2)}, u32[]{:S(2)}) async-start(bf16[32,48,2048]{2,1,0:T(8,128)(2,1)} %bitcast.180), calls=%async_computation | async-start | bytes 12582912 | tf_op jit(solution)/shard_map/all_to_all | solution.py:149
  232.8 79.4 %all-to-all-done = bf16[32,48,2048]{2,1,0:T(8,128)(2,1)} async-done(((bf16[32,48,2048]{2,1,0:T(8,128)(2,1)}), bf16[32,48,2048]{2,1,0:T(8,128)(2,1)}, u32[]{:S(2)}, u32[]{:S(2)}) %all-to-all-start) | async-done | bytes 6291488 | tf_op jit(solution)/shard_map/all_to_all | solution.py:149
  312.2 6.0 %fusion.26 = f32[32,48,256]{2,1,0:T(8,128)} fusion(bf16[32,48,2048]{2,1,0:T(8,128)(2,1)} %all-to-all-done, bf16[1,2048,256]{2,1,0:T(8,128)(2,1)S(1)} %copy-done.28), kind=kOutput, calls=%fused_computation.57 | convolution fusion | flops 1610612736 | bytes 8912896 | tf_op jit(solution)/shard_map/ncd,df->ncf/dot_general | solution.py:150
  318.2 12.8 %convolution_convert_fusion = bf16[32,48,2048]{2,1,0:T(8,128)(2,1)} fusion(f32[32,48,256]{2,1,0:T(8,128)} %fusion.26, bf16[32,48,2048]{2,1,0:T(8,128)(2,1)} %all-to-all-done, bf16[1,256,2048]{2,1,0:T(8,128)(2,1)S(1)} %copy-done.29, bf16[1,2048,256]{2,1,0:T(8,128)(2,1)} %param.29), kind=kOutput, calls=%fused_computation.17 | convolution fusion | flops 3226730496 | bytes 16252928 | tf_op jit(solution)/shard_map/ncf,fd->ncd/dot_general | solution.py:154
  331.0 5.0 all-to-all-start.1
  340.2 1.1 fusion.9
  341.3 4.6 rev.7
  345.9 68.0 %all-to-all-done.1 = bf16[32,48,2048]{2,1,0:T(8,128)(2,1)} async-done(((bf16[32,48,2048]{2,1,0:T(8,128)(2,1)}), bf16[32,48,2048]{2,1,0:T(8,128)(2,1)}, u32[]{:S(2)}, u32[]{:S(2)}) %all-to-all-start.1) | async-done | bytes 6291488 | tf_op jit(solution)/shard_map/all_to_all | solution.py:153
  414.0 6.0 %gather_fusion.7 = bf16[256,2048]{1,0:T(8,128)(2,1)S(1)} fusion(bf16[1536,2048]{1,0:T(8,128)(2,1)} %bitcast.22, s32[1024]{0:T(1024)S(1)} %pad_clamp_fusion), kind=kCustom, calls=%fused_computation.7 | custom fusion | bytes 2098176 | tf_op jit(solution)/shard_map/gather | solution.py:166
  419.9 6.0 %gather_fusion.6 = bf16[256,2048]{1,0:T(8,128)(2,1)S(1)} fusion(bf16[1536,2048]{1,0:T(8,128)(2,1)} %bitcast.22, s32[1024]{0:T(1024)S(1)} %pad_clamp_fusion.1), kind=kCustom, calls=%fused_computation.6 | custom fusion | bytes 2098176 | tf_op jit(solution)/shard_map/gather | solution.py:166
  425.9 6.0 %gather_fusion.5 = bf16[256,2048]{1,0:T(8,128)(2,1)S(1)} fusion(bf16[1536,2048]{1,0:T(8,128)(2,1)} %bitcast.22, s32[1024]{0:T(1024)S(1)} %pad_clamp_fusion.2), kind=kCustom, calls=%fused_computation.5 | custom fusion | bytes 2098176 | tf_op jit(solution)/shard_map/gather | solution.py:166
  431.9 7.1 %gather_fusion.4 = bf16[256,2048]{1,0:T(8,128)(2,1)} fusion(bf16[1536,2048]{1,0:T(8,128)(2,1)} %bitcast.22, s32[1024]{0:T(1024)} %pad_clamp_fusion.3), kind=kCustom, calls=%fused_computation.4 | custom fusion | bytes 2098176 | tf_op jit(solution)/shard_map/gather | solution.py:166
  439.0 7.3 %gather_fusion.3 = bf16[256,2048]{1,0:T(8,128)(2,1)} fusion(bf16[1536,2048]{1,0:T(8,128)(2,1)} %bitcast.22, s32[1024]{0:T(1024)} %pad_clamp_fusion.4), kind=kCustom, calls=%fused_computation.3 | custom fusion | bytes 2098176 | tf_op jit(solution)/shard_map/gather | solution.py:166
  446.3 7.1 %gather_fusion.2 = bf16[256,2048]{1,0:T(8,128)(2,1)} fusion(bf16[1536,2048]{1,0:T(8,128)(2,1)} %bitcast.22, s32[1024]{0:T(1024)} %pad_clamp_fusion.5), kind=kCustom, calls=%fused_computation.2 | custom fusion | bytes 2098176 | tf_op jit(solution)/shard_map/gather | solution.py:166
  453.4 7.1 %gather_fusion.1 = bf16[256,2048]{1,0:T(8,128)(2,1)} fusion(bf16[1536,2048]{1,0:T(8,128)(2,1)} %bitcast.22, s32[1024]{0:T(1024)} %pad_clamp_fusion.6), kind=kCustom, calls=%fused_computation.1 | custom fusion | bytes 2098176 | tf_op jit(solution)/shard_map/gather | solution.py:166
  460.4 7.0 %gather_fusion = bf16[256,2048]{1,0:T(8,128)(2,1)} fusion(bf16[1536,2048]{1,0:T(8,128)(2,1)} %bitcast.22, s32[1024]{0:T(1024)S(1)} %pad_clamp_fusion.7), kind=kCustom, calls=%fused_computation | custom fusion | bytes 2098176 | tf_op jit(solution)/shard_map/gather | solution.py:166
  467.4 4.7 add_convert_fusion
  472.1 52.9 %while.29 = (s32[]{:T(128)}, f32[2,128,128]{2,1,0:T(8,128)S(1)}, s32[]{:T(128)}, f32[32,2]{1,0:T(8,128)}, f32[32,2,128,128]{3,2,1,0:T(8,128)}, /*index=5*/s32[]{:T(128)}, s32[]{:T(128)}) while((s32[]{:T(128)}, f32[2,128,128]{2,1,0:T(8,128)S(1)}, s32[]{:T(128)}, f32[32,2]{1,0:T(8,128)}, f32[32,2,128,128]{3,2,1,0:T(8,128)}, ...), condition=%wide.region_15.16_spmd.clone, body=%wide.region_14.15_spmd.clone.sunk | while | flops 131076 | bytes 393353 | solution.py:31
  525.3 1.0 fusion.20
  526.3 1.8 copy.199
  528.2 1.2 fusion.16
  529.3 1.5 fusion.18
  531.9 1.5 fusion.19
  534.2 1.7 add_convert_fusion.1
  (231 shorter events, 72.4 us)
Async XLA Ops:
  7.2 2.2 copy-start
  7.2 66.8 %all-gather.8.cloned.1.call-start = ((), (), s32[]{:S(2)}) async-start(), calls=%async_computation.4 | async-start | bytes 4325376 | tf_op jit(solution)/shard_map/all_gather | solution.py:19
  9.4 4.8 copy-start.26
  9.4 6.0 %copy-start.18 = (f32[4,3,256]{2,0,1:T(4,128)S(1)}, f32[4,3,256]{2,0,1:T(4,128)}, u32[]{:S(2)}) copy-start(f32[4,3,256]{2,0,1:T(4,128)} %param.21) | copy-start | bytes 36868
  11.7 0.7 copy-start.12
  12.4 3.1 collective-permute-start
  15.2 29.7 %copy-start.23 = (f32[1,2,2,128]{3,1,2,0:T(2,128)}, f32[1,2,2,128]{3,1,2,0:T(2,128)S(1)}, u32[]{:S(2)}) copy-start(f32[1,2,2,128]{3,1,2,0:T(2,128)S(1)} %copy.239) | copy-start | bytes 6148
  17.2 56.7 %copy-start.8 = (bf16[256,2,128]{2,1,0:T(2,128)(2,1)}, bf16[256,2,128]{2,1,0:T(2,128)(2,1)S(1)}, u32[]{:S(2)}) copy-start(bf16[256,2,128]{2,1,0:T(2,128)(2,1)S(1)} %convert_element_type.121) | copy-start | bytes 393220
  17.4 27.4 %copy-start.10 = (bf16[256,2,128]{0,2,1:T(8,128)(2,1)}, bf16[256,2,128]{0,2,1:T(8,128)(2,1)S(1)}, u32[]{:S(2)}) copy-start(bf16[256,2,128]{0,2,1:T(8,128)(2,1)S(1)} %copy.176) | copy-start | bytes 393220
  18.3 182.4 %all-gather.10.cloned.1.call-start = ((), (), s32[]{:S(2)}) async-start(), calls=%async_computation.5 | async-start | bytes 9437184 | tf_op jit(solution)/shard_map/all_gather | solution.py:129
  44.0 0.6 copy-start.19
  44.7 29.3 %copy-start.15 = (pred[256,256]{1,0:T(8,128)(4,1)}, pred[256,256]{1,0:T(8,128)(4,1)S(1)}, u32[]{:S(2)}) copy-start(pred[256,256]{1,0:T(8,128)(4,1)S(1)} %iota_compare_fusion.1) | copy-start | bytes 196612
  44.9 187.0 %copy-start.5 = (bf16[256,1,256]{0,2,1:T(8,128)(2,1)}, bf16[256,1,256]{0,2,1:T(8,128)(2,1)S(1)}, u32[]{:S(2)}) copy-start(bf16[256,1,256]{0,2,1:T(8,128)(2,1)S(1)} %copy.207) | copy-start | bytes 393220
  45.2 62.0 %copy-start.3 = (f32[2,256,256]{2,1,0:T(8,128)}, f32[2,256,256]{2,1,0:T(8,128)S(1)}, u32[]{:S(2)}) copy-start(f32[2,256,256]{2,1,0:T(8,128)S(1)} %convolution_multiply_fusion) | copy-start | bytes 1572868
  45.2 61.8 %copy-start.27 = (f32[256]{0:T(256)S(1)}, f32[256]{0:T(256)}, u32[]{:S(2)}) copy-start(f32[256]{0:T(256)} %param.23) | copy-start | bytes 3076
  74.0 33.2 %copy-start.11 = (bf16[256,2048]{1,0:T(8,128)(2,1)S(1)}, bf16[256,2048]{1,0:T(8,128)(2,1)}, u32[]{:S(2)}) copy-start(bf16[256,2048]{1,0:T(8,128)(2,1)} %param.24) | copy-start | bytes 3145732
  107.0 1.7 copy-start.13
  107.2 2.7 copy-start.22
  200.7 5.3 copy-start.2
  206.0 1.7 copy-start.21
  224.1 7.6 %copy-start.14 = (bf16[256,256]{1,0:T(8,128)(2,1)S(1)}, bf16[256,256]{1,0:T(8,128)(2,1)}, u32[]{:S(2)}) copy-start(bf16[256,256]{1,0:T(8,128)(2,1)} %param.31) | copy-start | bytes 393220
  224.1 88.1 %copy-start.28 = (bf16[1,2048,256]{2,1,0:T(8,128)(2,1)S(1)}, bf16[1,2048,256]{2,1,0:T(8,128)(2,1)}, u32[]{:S(2)}) copy-start(bf16[1,2048,256]{2,1,0:T(8,128)(2,1)} %param.28) | copy-start | bytes 3145732
  224.1 88.1 %all-to-all-start = ((bf16[32,48,2048]{2,1,0:T(8,128)(2,1)}), bf16[32,48,2048]{2,1,0:T(8,128)(2,1)}, u32[]{:S(2)}, u32[]{:S(2)}) async-start(bf16[32,48,2048]{2,1,0:T(8,128)(2,1)} %bitcast.180), calls=%async_computation | async-start | bytes 12582912 | tf_op jit(solution)/shard_map/all_to_all | solution.py:149
  231.5 109.8 %all-gather.12.cloned.1.call-start = ((), (), s32[]{:S(2)}) async-start(), calls=%async_computation.6 | async-start | bytes 4325376 | tf_op jit(solution)/shard_map/all_gather | solution.py:19
  231.8 108.4 %copy-start.6 = (bf16[256,256]{0,1:T(8,128)(2,1)}, bf16[256,256]{0,1:T(8,128)(2,1)S(1)}, u32[]{:S(2)}) copy-start(bf16[256,256]{0,1:T(8,128)(2,1)S(1)} %copy.208) | copy-start | bytes 393220
  232.8 85.4 %copy-start.29 = (bf16[1,256,2048]{2,1,0:T(8,128)(2,1)S(1)}, bf16[1,256,2048]{2,1,0:T(8,128)(2,1)}, u32[]{:S(2)}) copy-start(bf16[1,256,2048]{2,1,0:T(8,128)(2,1)} %param.30) | copy-start | bytes 3145732
  331.0 5.3 copy-start.20
  331.0 8.6 %copy-start.17 = (f32[256,8]{0,1:T(8,128)S(1)}, f32[256,8]{0,1:T(8,128)}, u32[]{:S(2)}) copy-start(f32[256,8]{0,1:T(8,128)} %get-tuple-element.336) | copy-start | bytes 24580
  331.0 9.2 %copy-start.16 = (pred[256,256]{1,0:T(8,128)(4,1)S(1)}, pred[256,256]{1,0:T(8,128)(4,1)}, u32[]{:S(2)}) copy-start(pred[256,256]{1,0:T(8,128)(4,1)} %copy-done.15) | copy-start | bytes 196612
  331.0 9.2 %copy-start.24 = (f32[1,2,2,128]{3,1,2,0:T(2,128)S(1)}, f32[1,2,2,128]{3,1,2,0:T(2,128)}, u32[]{:S(2)}) copy-start(f32[1,2,2,128]{3,1,2,0:T(2,128)} %copy-done.23) | copy-start | bytes 6148
  331.0 83.0 %all-to-all-start.1 = ((bf16[32,48,2048]{2,1,0:T(8,128)(2,1)}), bf16[32,48,2048]{2,1,0:T(8,128)(2,1)}, u32[]{:S(2)}, u32[]{:S(2)}) async-start(bf16[32,48,2048]{2,1,0:T(8,128)(2,1)} %convolution_convert_fusion), calls=%async_computation.1 | async-start | bytes 12582912 | tf_op jit(solution)/shard_map/all_to_all | solution.py:153
  336.1 198.1 %reduce-scatter.2.cloned.1.call-start = ((), (), s32[]{:S(2)}) async-start(), calls=%async_computation.3 | async-start | bytes 1179648 | tf_op jit(solution)/shard_map/reduce_scatter | solution.py:167
  460.4 7.0 %copy-start.25 = (f32[256,1]{0,1:T(1,128)S(1)}, f32[256,1]{0,1:T(1,128)}, u32[]{:S(2)}) copy-start(f32[256,1]{0,1:T(1,128)} %get-tuple-element.350) | copy-start | bytes 3076
  472.1 52.9 %copy-start.9 = (bf16[256,2,128]{2,1,0:T(2,128)(2,1)S(1)}, bf16[256,2,128]{2,1,0:T(2,128)(2,1)}, u32[]{:S(2)}) copy-start(bf16[256,2,128]{2,1,0:T(2,128)(2,1)} %copy-done.8) | copy-start | bytes 393220
  472.1 53.3 %copy-start.4 = (f32[2,256,256]{2,1,0:T(8,128)S(1)}, f32[2,256,256]{2,1,0:T(8,128)}, u32[]{:S(2)}) copy-start(f32[2,256,256]{2,1,0:T(8,128)} %copy-done.3) | copy-start | bytes 1572868
  472.1 53.3 %copy-start.7 = (bf16[256,256]{0,1:T(8,128)(2,1)S(1)}, bf16[256,256]{0,1:T(8,128)(2,1)}, u32[]{:S(2)}) copy-start(bf16[256,256]{0,1:T(8,128)(2,1)} %copy-done.6) | copy-start | bytes 393220
  526.3 9.5 %copy-start.1 = (bf16[2048,3,256]{2,0,1:T(8,128)(2,1)S(1)}, bf16[2048,3,256]{2,0,1:T(8,128)(2,1)}, u32[]{:S(2)}) copy-start(bf16[2048,3,256]{2,0,1:T(8,128)(2,1)} %param.20) | copy-start | bytes 9437188
Sparse Core Ops, SparseCore 0:
  18.4 55.4 all-gather.7
  108.9 91.7 all-gather.9
  235.4 87.3 all-gather.11
  472.2 35.2 reduce-scatter.1
